TPU v7x, 32 devices: a whole 2x2x4 slice. The times are simulated.
32 devices in a mesh: dp: 2 (over y), seq: 4 (over z), chan: 4 (over x, core).
Axes of the slice: x: 2, y: 2, z: 4, core: 2. Of those that a mesh axis runs over, the one named last changes fastest.
Arguments:
- tokens: bfloat16 [16384, 1024], P(('dp', 'seq'), 'chan'), may hold values from -6 to 6
- gain_one: bfloat16 [1024], P('chan'), may hold values from 0.25 to 1.75
- in_weight: bfloat16 [1024, 3, 1024], P(None, None, 'chan'), may hold values from -0.1875 to 0.1875
- conv_weight: bfloat16 [3, 1024], P(None, 'chan'), may hold values from -3 to 3
- out_weight: bfloat16 [1024, 1024], P('chan'), may hold values from -0.1875 to 0.1875
- gain_two: bfloat16 [1024], replicated, may hold values from 0.25 to 1.75
- gate_up_weight: bfloat16 [1024, 2, 4608], P(None, None, 'chan'), may hold values from -0.1875 to 0.1875
- down_weight: bfloat16 [4608, 1024], P('chan'), may hold values from -0.09375 to 0.09375
- cotangent: bfloat16 [16384, 1024], P(('dp', 'seq'), 'chan'), may hold values from -6 to 6
Outputs:
- result: bfloat16 [16384, 1024], P(('dp', 'seq'), 'chan')
- grad_tokens: bfloat16 [16384, 1024], P(('dp', 'seq'), 'chan')
- grad_gain_one: float32 [1024], P('chan')
- grad_in_weight: float32 [1024, 3, 1024], P(None, None, 'chan')
- grad_conv_weight: float32 [3, 1024], P(None, 'chan')
- grad_out_weight: float32 [1024, 1024], P('chan')
- grad_gain_two: float32 [1024], P('chan')
- grad_gate_up: float32 [1024, 2, 4608], P(None, None, 'chan')
- grad_down: float32 [4608, 1024], P('chan')
All inputs are finite; a program needn't handle non-finite values.
Results may differ from a plain program's by a relative error of at most 0.018.
Values may be sent and summed in bfloat16 or wider, within the bound.
No kernel may reach another device: no remote copies, remote signals or barrier semaphores. Data moves between devices by JAX's collectives and lax.ppermute only.
A program may use at most 256 MiB of HBM per device.

v0:
```python
import jax
import jax.numpy as jnp
from jax import lax
from jax.sharding import PartitionSpec as P

epsilon = 1e-05


def shifted(value, axis, by):
    length = lax.axis_size(axis)
    pairs = [(i, i + by) for i in range(length) if 0 <= i + by < length]
    return lax.ppermute(value, axis, pairs)


def shards(
    tokens,
    gain_one,
    in_weight,
    conv_weight,
    out_weight,
    gain_two,
    gate_up_weight,
    down_weight,
    cotangent,
):
    width = in_weight.shape[0]
    local_width = in_weight.shape[2]
    hidden_local = gate_up_weight.shape[2]
    count = tokens.shape[0]
    offset = lax.axis_index("chan") * local_width
    in_flat = in_weight.reshape(width, 3 * local_width)
    gu_flat = gate_up_weight.reshape(width, 2 * hidden_local)
    kernel = conv_weight.astype(jnp.float32)
    gain_second = gain_two.astype(jnp.float32)
    tokens_local = tokens.astype(jnp.float32)
    tokens_full, gain_full = (
        lax.all_gather(tokens, "chan", axis=1, tiled=True),
        lax.all_gather(gain_one, "chan", axis=0, tiled=True),
    )
    x_float = tokens_full.astype(jnp.float32)
    inv_one = lax.rsqrt(jnp.mean(x_float * x_float, axis=-1, keepdims=True) + epsilon)
    normed_one = (x_float * inv_one * gain_full.astype(jnp.float32)).astype(jnp.bfloat16)
    projected = jnp.dot(normed_one, in_flat, preferred_element_type=jnp.float32)
    gate_b = projected[:, :local_width]
    gate_c = projected[:, local_width : 2 * local_width]
    values = projected[:, 2 * local_width :]
    product = gate_b * values
    state = shifted(product[count - 2 :], "seq", 1)
    extended = jnp.concatenate([state, product], axis=0)
    conv_out = (
        kernel[0] * extended[0:count]
        + kernel[1] * extended[1 : count + 1]
        + kernel[2] * extended[2 : count + 2]
    )
    mixed = (gate_c * conv_out).astype(jnp.bfloat16)
    mix_partial = jnp.dot(mixed, out_weight, preferred_element_type=jnp.float32)
    resid = x_float + lax.psum(mix_partial, "chan")
    inv_two = lax.rsqrt(jnp.mean(resid * resid, axis=-1, keepdims=True) + epsilon)
    scaled_two = resid * inv_two
    normed_two = (scaled_two * gain_second).astype(jnp.bfloat16)
    resid_local = lax.dynamic_slice_in_dim(resid, offset, local_width, 1)
    gate_up = jnp.dot(normed_two, gu_flat, preferred_element_type=jnp.float32)
    gate_pre = gate_up[:, :hidden_local]
    up_pre = gate_up[:, hidden_local:]
    sigma = jax.nn.sigmoid(gate_pre)
    hidden = (gate_pre * sigma * up_pre).astype(jnp.bfloat16)
    ffn_local = lax.psum_scatter(
        jnp.dot(hidden, down_weight, preferred_element_type=jnp.float32).astype(jnp.bfloat16),
        "chan",
        scatter_dimension=1,
        tiled=True,
    ).astype(jnp.float32)
    result = (resid_local + ffn_local).astype(jnp.bfloat16)
    cot_full = lax.all_gather(cotangent, "chan", axis=1, tiled=True)
    d_hidden = jnp.dot(cot_full, down_weight.T, preferred_element_type=jnp.float32)
    grad_down = jnp.dot(hidden.T, cot_full, preferred_element_type=jnp.float32)
    d_gate = d_hidden * up_pre * sigma * (1.0 + gate_pre * (1.0 - sigma))
    d_up = d_hidden * gate_pre * sigma
    d_gate_up = jnp.concatenate([d_gate, d_up], axis=1).astype(jnp.bfloat16)
    grad_gate_up = jnp.dot(normed_two.T, d_gate_up, preferred_element_type=jnp.float32).reshape(
        width, 2, hidden_local
    )
    norm_partial = jnp.dot(d_gate_up, gu_flat.T, preferred_element_type=jnp.float32)
    d_norm_two = lax.psum(norm_partial, "chan")
    grad_gain_two = lax.dynamic_slice_in_dim(
        jnp.sum(d_norm_two * scaled_two, axis=0), offset, local_width, 0
    )
    pulled_two = d_norm_two * gain_second
    d_resid = cot_full.astype(jnp.float32) + inv_two * (
        pulled_two - scaled_two * jnp.mean(pulled_two * scaled_two, axis=-1, keepdims=True)
    )
    d_out = d_resid.astype(jnp.bfloat16)
    d_resid_local = lax.dynamic_slice_in_dim(d_resid, offset, local_width, 1)
    d_mixed = jnp.dot(d_out, out_weight.T, preferred_element_type=jnp.float32)
    grad_out = jnp.dot(mixed.T, d_out, preferred_element_type=jnp.float32)
    d_gate_c = d_mixed * conv_out
    d_conv = d_mixed * gate_c
    next_grad = shifted(d_conv[0:2], "seq", -1)
    grad_ext = jnp.concatenate([d_conv, next_grad], axis=0)
    d_product = (
        kernel[2] * grad_ext[0:count]
        + kernel[1] * grad_ext[1 : count + 1]
        + kernel[0] * grad_ext[2 : count + 2]
    )
    grad_conv = jnp.stack(
        [
            jnp.sum(d_conv * extended[shift_index : shift_index + count], axis=0)
            for shift_index in range(3)
        ]
    )
    d_project = jnp.concatenate([d_product * values, d_gate_c, d_product * gate_b], axis=1).astype(
        jnp.bfloat16
    )
    grad_in = jnp.dot(normed_one.T, d_project, preferred_element_type=jnp.float32).reshape(
        width, 3, local_width
    )
    d_norm_one = lax.psum_scatter(
        jnp.dot(d_project, in_flat.T, preferred_element_type=jnp.float32).astype(jnp.bfloat16),
        "chan",
        scatter_dimension=1,
        tiled=True,
    ).astype(jnp.float32)
    scaled_one = tokens_local * inv_one
    grad_gain_one = jnp.sum(d_norm_one * scaled_one, axis=0)
    pulled_one = d_norm_one * gain_one.astype(jnp.float32)
    inner_sum = lax.psum(jnp.sum(pulled_one * scaled_one, axis=-1, keepdims=True), "chan")
    grad_tokens = (
        d_resid_local + inv_one * (pulled_one - scaled_one * (inner_sum / width))
    ).astype(jnp.bfloat16)
    grad_gain_one, grad_in, grad_conv, grad_out, grad_gain_two, grad_gate_up, grad_down = (
        lax.psum(grad_gain_one.astype(jnp.bfloat16), ("dp", "seq")).astype(jnp.float32),
        lax.psum(grad_in.astype(jnp.bfloat16), ("dp", "seq")).astype(jnp.float32),
        lax.psum(grad_conv.astype(jnp.bfloat16), ("dp", "seq")).astype(jnp.float32),
        lax.psum(grad_out.astype(jnp.bfloat16), ("dp", "seq")).astype(jnp.float32),
        lax.psum(grad_gain_two.astype(jnp.bfloat16), ("dp", "seq")).astype(jnp.float32),
        lax.psum(grad_gate_up.astype(jnp.bfloat16), ("dp", "seq")).astype(jnp.float32),
        lax.psum(grad_down.astype(jnp.bfloat16), ("dp", "seq")).astype(jnp.float32),
    )
    return (
        result,
        grad_tokens,
        grad_gain_one,
        grad_in,
        grad_conv,
        grad_out,
        grad_gain_two,
        grad_gate_up,
        grad_down,
    )


def solution(mesh):
    placed = (
        P(("dp", "seq"), "chan"),
        P("chan"),
        P(None, None, "chan"),
        P(None, "chan"),
        P("chan", None),
        P(),
        P(None, None, "chan"),
        P("chan", None),
        P(("dp", "seq"), "chan"),
    )
    return jax.shard_map(
        shards,
        mesh=mesh,
        in_specs=placed,
        out_specs=(
            P(("dp", "seq"), "chan"),
            P(("dp", "seq"), "chan"),
            P("chan"),
            P(None, None, "chan"),
            P(None, "chan"),
            P("chan", None),
            P("chan"),
            P(None, None, "chan"),
            P("chan", None),
        ),
        check_vma=False,
    )
```

profile of v0, /device:TPU:0, one launch (start us, length us, event | category | flops | bytes accessed | tf_op | source)
XLA Modules:
  0.0 858.1 jit_solution(401732263966881372)
XLA Ops:
  10.6 6.0 all-gather
  16.6 30.7 %all-gather.4.cloned.1.call-done = bf16[2048,1024]{1,0:T(8,128)(2,1)} async-done(((bf16[2048,256]{1,0:T(8,128)(2,1)}), bf16[2048,1024]{1,0:T(8,128)(2,1)}) %all-gather.4.cloned.1.call-update) | async-done | bytes 4194320 | tf_op jit(solution)/shard_map/all_gather | solution.py:37
  47.3 3.2 fusion
  50.8 5.0 fusion.27
  56.1 3.5 collective-permute-start
  64.0 4.7 fusion.36
  69.8 5.4 copy.30
  75.1 147.3 %all-reduce.6.cloned.1.call-done = f32[2048,1024]{1,0:T(8,128)} async-done(((f32[2048,1024]{1,0:T(8,128)}), f32[2048,1024]{1,0:T(8,128)}) %all-reduce.6.cloned.1.call-update) | async-done | bytes 8388624 | tf_op jit(solution)/shard_map/psum | solution.py:57
  222.5 5.7 multiply_reduce_fusion.2
  228.2 3.4 copy-done.3
  231.6 16.3 %fusion.33 = f32[2048,2304]{1,0:T(8,128)} fusion(bf16[1024,2304]{1,0:T(8,128)(2,1)} %bitcast.27, f32[2048,1024]{1,0:T(8,128)S(1)} %get-tuple-element.27, f32[1024]{0:T(1024)S(1)} %convert_element_type.107, f32[2048]{0:T(1024)S(1)} %add_rsqrt_fusion), kind=kOutput, calls=%fused_computation.73 | convolution fusion | flops 9669967872 | bytes 31993856 | tf_op jit(solution)/shard_map/dot_general | solution.py:62
  247.9 11.3 %all-gather.6.cloned.1.call-done = bf16[2048,1024]{1,0:T(8,128)(2,1)} async-done(((bf16[2048,256]{1,0:T(8,128)(2,1)}), bf16[2048,1024]{1,0:T(8,128)(2,1)}) %all-gather.6.cloned.1.call-update) | async-done | bytes 4194320 | tf_op jit(solution)/shard_map/all_gather | solution.py:74
  259.2 18.2 %multiply_convert_fusion.1 = (bf16[2048,1152]{1,0:T(8,128)(2,1)}, bf16[2048,1152]{1,0:T(8,128)(2,1)}, bf16[2048,1152]{1,0:T(8,128)(2,1)}) fusion(f32[2048,2304]{1,0:T(8,128)} %fusion.33, bf16[2048,1024]{1,0:T(8,128)(2,1)} %all-gather.6.cloned.1.call-done, bf16[1152,1024]{1,0:T(8,128)(2,1)S(1)} %copy-done), kind=kOutput, calls=%fused_computation.5 | convolution fusion | flops 4869586944 | bytes 39583744 | tf_op jit(solution)/shard_map/dot_general | solution.py:75
  277.4 15.8 %fusion.4 = f32[2048,1024]{1,0:T(8,128)} fusion(bf16[1024,2304]{1,0:T(8,128)(2,1)} %bitcast.28, bf16[2048,1152]{1,0:T(8,128)(2,1)} %get-tuple-element.31, bf16[2048,1152]{1,0:T(8,128)(2,1)} %get-tuple-element.30), kind=kOutput, calls=%fused_computation.17 | convolution fusion | flops 9682550784 | bytes 22544384 | tf_op jit(solution)/shard_map/dot_general | solution.py:83
  293.9 9.5 %convolution_convert_fusion.1 = bf16[2048,1024]{1,0:T(8,128)(2,1)} fusion(bf16[2048,1152]{1,0:T(8,128)(2,1)} %get-tuple-element.32, bf16[1152,1024]{1,0:T(8,128)(2,1)S(1)} %copy-done), kind=kOutput, calls=%fused_computation.20 | convolution fusion | flops 4833935360 | bytes 11272192 | tf_op jit(solution)/shard_map/dot_general | solution.py:68
  303.5 142.9 %all-reduce.8.cloned.1.call-done = f32[2048,1024]{1,0:T(8,128)} async-done(((f32[2048,1024]{1,0:T(8,128)}), f32[2048,1024]{1,0:T(8,128)}) %all-reduce.8.cloned.1.call-update) | async-done | bytes 8388624 | tf_op jit(solution)/shard_map/psum | solution.py:84
  446.3 7.1 multiply_reduce_fusion
  454.9 7.7 multiply_add_fusion
  470.7 4.2 collective-permute-done.1
  477.8 5.0 convolution_convert_fusion.2
  483.0 16.9 %fusion.5 = bf16[1024,2304]{1,0:T(8,128)(2,1)} fusion(bf16[2048,1152]{1,0:T(8,128)(2,1)} %get-tuple-element.31, bf16[2048,1152]{1,0:T(8,128)(2,1)} %get-tuple-element.30, f32[2048,1024]{1,0:T(8,128)} %copy-done.3, f32[1024]{0:T(1024)S(1)} %convert_element_type.107, f32[2048]{0:T(1024)S(1)} %add_rsqrt_fusion), kind=kOutput, calls=%fused_computation.18 | convolution fusion | flops 9691201536 | bytes 22556672 | tf_op jit(solution)/shard_map/dot_general | solution.py:80
  500.0 10.3 %convert_element_type.131 = bf16[1024,2,1152]{2,1,0:T(2,128)(2,1)} reshape(bf16[1024,2304]{1,0:T(8,128)(2,1)} %fusion.5) | data formatting | bytes 9437184 | tf_op jit(solution)/shard_map/convert_element_type | solution.py:136
  510.3 9.6 %convolution_convert_fusion = bf16[1152,1024]{1,0:T(8,128)(2,1)} fusion(bf16[2048,1152]{1,0:T(8,128)(2,1)} %get-tuple-element.32, bf16[2048,1024]{1,0:T(8,128)(2,1)} %all-gather.6.cloned.1.call-done), kind=kOutput, calls=%fused_computation.19 | convolution fusion | flops 4833017856 | bytes 11272192 | tf_op jit(solution)/shard_map/dot_general | solution.py:76
  519.9 5.6 fusion.23
  525.6 4.0 convolution_convert_fusion.3
  531.9 3.2 add_convert_fusion
  535.1 5.0 reduce-scatter.5.cloned.1.call-done
  542.2 22.3 %all-reduce = (bf16[256]{0:T(256)(128)(2,1)S(1)}, bf16[3,256]{1,0:T(4,128)(2,1)S(1)}, bf16[256]{0:T(256)(128)(2,1)S(1)}) all-reduce(bf16[256]{0:T(256)(128)(2,1)S(1)} %get-tuple-element.14, bf16[3,256]{1,0:T(4,128)(2,1)S(1)} %pad_maximum_fusion.10, ...), channel_id=1, replica_groups=mesh['dp'=2,'seq'=4,'chan'=4] {'dp','seq'}, use_global_device_ids=true, to_apply=%region_10.0 | all-reduce | flops 1280 | bytes 5120 | tf_op jit(solution)/shard_map/psum | solution.py:131
  566.3 6.1 psum.72
  572.4 3.1 fusion.16
  575.6 262.1 %all-reduce.10.cloned.1.call-done = (bf16[1024,3,256]{2,0,1:T(8,128)(2,1)}, bf16[256,1024]{1,0:T(8,128)(2,1)}, bf16[1024,2,1152]{2,1,0:T(2,128)(2,1)}, bf16[1152,1024]{1,0:T(8,128)(2,1)}) async-done(((bf16[1024,3,256]{2,0,1:T(8,128)(2,1)}, bf16[256,1024]{1,0:T(8,128)(2,1)}, bf16[1024,2,1152]{2,1,0:T(2,128)(2,1)}, bf16[1152,1024]{1,0:T(8,128)(2,1)}), (bf16[1024,3,256]{2,0,1:T(8,128)(2,1)}, ...) | async-done | bytes 9175056 | tf_op jit(solution)/shard_map/psum | solution.py:132
  837.7 7.3 convert_element_type.132
  (114 shorter events, 34.7 us)
Async XLA Ops:
  7.2 252.0 %copy-start = (bf16[1152,1024]{1,0:T(8,128)(2,1)S(1)}, bf16[1152,1024]{1,0:T(8,128)(2,1)}, u32[]{:S(2)}) copy-start(bf16[1152,1024]{1,0:T(8,128)(2,1)} %param.16) | copy-start | bytes 7077892
  7.2 40.1 %all-gather.4.cloned.1.call-start = ((), (), s32[]{:S(2)}) async-start(), calls=%async_computation.2 | async-start | bytes 5242880 | tf_op jit(solution)/shard_map/all_gather | solution.py:37
  7.9 214.5 %all-reduce.6.cloned.1.call-start = ((), (), s32[]{:S(2)}) async-start(), calls=%async_computation.3 | async-start | bytes 16777216 | tf_op jit(solution)/shard_map/psum | solution.py:57
  16.6 39.2 %copy-start.26 = (f32[4,1,256]{2,1,0:T(1,128)}, f32[4,1,256]{2,1,0:T(1,128)S(1)}, u32[]{:S(2)}) copy-start(f32[4,1,256]{2,1,0:T(1,128)S(1)} %convert_element_type.135) | copy-start | bytes 12292
  50.6 5.2 copy-start.23
  55.8 7.2 copy-start.5
  55.8 3.9 copy-start.25
  56.1 6.9 copy-start.6
  56.1 7.9 copy-start.15
  56.1 4.8 collective-permute-start
  68.7 190.5 %all-gather.6.cloned.1.call-start = ((), (), s32[]{:S(2)}) async-start(), calls=%async_computation.5 | async-start | bytes 5242880 | tf_op jit(solution)/shard_map/all_gather | solution.py:74
  69.4 376.9 %all-reduce.8.cloned.1.call-start = ((), (), s32[]{:S(2)}) async-start(), calls=%async_computation.6 | async-start | bytes 16777216 | tf_op jit(solution)/shard_map/psum | solution.py:84
  293.3 238.6 %reduce-scatter.3.cloned.1.call-start = ((), (), s32[]{:S(2)}) async-start(), calls=%async_computation.4 | async-start | bytes 5242880 | tf_op jit(solution)/shard_map/reduce_scatter | solution.py:67
  303.4 236.7 %reduce-scatter.5.cloned.1.call-start = ((), (), s32[]{:S(2)}) async-start(), calls=%async_computation.7 | async-start | bytes 5242880 | tf_op jit(solution)/shard_map/reduce_scatter | solution.py:117
  446.3 8.5 copy-start.4
  446.3 20.5 %slice-start = ((s8[6291456]{0:T(1024)(128)(4,1)}), s8[4194304]{0:T(1024)(128)(4,1)S(1)}, s32[]{:S(2)}) async-start(s8[6291456]{0:T(1024)(128)(4,1)} %bitcast.24), calls=%async_computation.9 | async-start | bytes 8388608
  454.9 12.0 %slice-start.1 = ((s8[6291456]{0:T(1024)(128)(4,1)}), s8[2097152]{0:T(1024)(128)(4,1)S(1)}, s32[]{:S(2)}) async-start(s8[6291456]{0:T(1024)(128)(4,1)} %bitcast.24), calls=%async_computation.10 | async-start | bytes 4194304
  462.6 4.3 copy-start.2
  462.6 4.3 copy-start.7
  462.6 5.6 copy-start.13
  469.4 5.5 collective-permute-start.1
  482.8 354.9 %all-reduce.10.cloned.1.call-start = ((), (), s32[]{:S(2)}) async-start(), calls=%async_computation.8 | async-start | bytes 18350080 | tf_op jit(solution)/shard_map/psum | solution.py:132
  510.3 9.6 %copy-start.11 = (bf16[2048,256]{1,0:T(8,128)(2,1)S(1)}, bf16[2048,256]{1,0:T(8,128)(2,1)}, u32[]{:S(2)}) copy-start(bf16[2048,256]{1,0:T(8,128)(2,1)} %copy-done.10) | copy-start | bytes 3145732
  519.8 5.7 copy-start.9
  519.9 5.7 copy-start.19
  519.9 5.7 copy-start.21
  519.9 5.7 copy-start.24
  519.9 5.7 copy-start.27
  531.8 8.3 copy-start.12
  837.7 7.3 copy-start.14
  845.0 4.9 copy-start.22
  845.0 6.0 copy-start.1
  (10 other events, 20.1 us)
Sparse Core Ops, SparseCore 0:
  9.6 37.7 all-gather.3
  68.8 153.6 all-reduce.5
  224.0 35.1 all-gather.5
  293.4 152.8 all-reduce.7
  448.7 44.5 reduce-scatter.2
  495.7 44.3 reduce-scatter.4
  545.9 291.7 all-reduce.9
where the time goes:
time: 864 us; the launch traced here: 858 us
  waiting for transfers between devices  606 us (70%)
  matrix products  114 us (13%)
  other arithmetic  51.8 us (6%)
  blocking collectives  34.5 us (4%)
  local copies, waits for them, and re-layouts  31.2 us (4%)
  between operations  14.8 us (2%)
    psum x1, waiting for transfers between devices, shards(): lax.psum(grad_in.astype(jnp.bfloat16), ('dp', 'seq')).astype(jnp.float32)  262 us
    psum x1, waiting for transfers between devices, shards(): resid = x_float + lax.psum(mix_partial, 'chan')  147 us
    psum x1, waiting for transfers between devices, shards(): d_norm_two = lax.psum(norm_partial, 'chan')  143 us
    all_gather x1, waiting for transfers between devices, shards(): lax.all_gather(tokens, 'chan', axis=1, tiled=True)  30.7 us
    psum x1, blocking collectives, shards(): lax.psum(grad_gain_one.astype(jnp.bfloat16), ('dp', 'seq'))  22.3 us
    unnamed x69, local copies, waits for them, and re-layouts  19.2 us
    dot_general x1, matrix products, shards(): jnp.dot(cot_full, down_weight.T, preferred_element_type=jnp.float32)  18.2 us
  transfers between devices with their start and end apart: 9, of which 8 were waited for; matrix products, arithmetic and copies ran while one was open for 14% of the time, Pallas kernels for 0%

commit v1 on v0

--- a/solution.py
+++ b/solution.py
@@ -129,7 +129,7 @@
     ).astype(jnp.bfloat16)
     grad_gain_one, grad_in, grad_conv, grad_out, grad_gain_two, grad_gate_up, grad_down = (
         lax.psum(grad_gain_one.astype(jnp.bfloat16), ("dp", "seq")).astype(jnp.float32),
-        lax.psum(grad_in.astype(jnp.bfloat16), ("dp", "seq")).astype(jnp.float32),
+        lax.psum(lax.psum(grad_in.astype(jnp.bfloat16), "dp"), "seq").astype(jnp.float32),
         lax.psum(grad_conv.astype(jnp.bfloat16), ("dp", "seq")).astype(jnp.float32),
         lax.psum(grad_out.astype(jnp.bfloat16), ("dp", "seq")).astype(jnp.float32),
         lax.psum(grad_gain_two.astype(jnp.bfloat16), ("dp", "seq")).astype(jnp.float32),

time: 864 us -> 1000 us (1.16)
  waiting for transfers between devices: 606 us -> 739 us
    psum x1 -> x3, waiting for transfers between devices: 262 us -> 312 us  [the longest x1 251 us: shards(): lax.psum(grad_out.astype(jnp.bfloat16), ('dp', 'seq')).astype(jnp.float32)]
    reduce_scatter x1, waiting for transfers between devices: 0.02 us -> 42.8 us  [shards(): lax.psum_scatter(jnp.dot(hidden, down_weight, preferred_element_type=jnp....]
    reduce_scatter x1, waiting for transfers between devices: 4.97 us -> 34.8 us  [shards(): lax.psum_scatter(jnp.dot(d_project, in_flat.T, preferred_element_type=jnp...]
  transfers between devices with their start and end apart: 9 -> 11, of which waited for: 8 -> 11; matrix products, arithmetic and copies ran while one was open for 14% -> 11% of each run, Pallas kernels for 0% -> 0%
where the time goes in v1:
time: 1000 us; the launch traced here: 993 us
  waiting for transfers between devices  739 us (74%)
  matrix products  117 us (12%)
  other arithmetic  51.1 us (5%)
  blocking collectives  33.6 us (3%)
  local copies, waits for them, and re-layouts  32.3 us (3%)
  between operations  14.4 us (1%)
    psum x1, waiting for transfers between devices, shards(): lax.psum(grad_out.astype(jnp.bfloat16), ('dp', 'seq')).astype(jnp.float32)  251 us
    psum x1, waiting for transfers between devices, shards(): d_norm_two = lax.psum(norm_partial, 'chan')  153 us
    psum x1, waiting for transfers between devices, shards(): resid = x_float + lax.psum(mix_partial, 'chan')  147 us
    psum x1, waiting for transfers between devices, shards(): lax.psum(grad_in.astype(jnp.bfloat16), 'dp')  50.9 us
    reduce_scatter x1, waiting for transfers between devices, shards(): lax.psum_scatter(jnp.dot(hidden, down_weight, preferred_element_type=jnp....  42.8 us
    reduce_scatter x1, waiting for transfers between devices, shards(): lax.psum_scatter(jnp.dot(d_project, in_flat.T, preferred_element_type=jnp...  34.8 us
    all_gather x1, waiting for transfers between devices, shards(): lax.all_gather(tokens, 'chan', axis=1, tiled=True)  30.7 us
    psum x1, blocking collectives, shards(): lax.psum(grad_gain_one.astype(jnp.bfloat16), ('dp', 'seq'))  21.5 us
  transfers between devices with their start and end apart: 11, of which 11 were waited for; matrix products, arithmetic and copies ran while one was open for 11% of the time, Pallas kernels for 0%

profile of v1, /device:TPU:0, one launch (start us, length us, event | category | flops | bytes accessed | tf_op | source)
XLA Modules:
  0.0 993.3 jit_solution(1072018315920068617)
XLA Ops:
  10.6 6.0 all-gather
  16.6 30.7 %all-gather.4.cloned.1.call-done = bf16[2048,1024]{1,0:T(8,128)(2,1)} async-done(((bf16[2048,256]{1,0:T(8,128)(2,1)}), bf16[2048,1024]{1,0:T(8,128)(2,1)}) %all-gather.4.cloned.1.call-update) | async-done | bytes 4194320 | tf_op jit(solution)/shard_map/all_gather | solution.py:37
  50.8 5.0 fusion.27
  56.1 3.5 collective-permute-start
  64.0 4.7 fusion.36
  70.0 5.5 copy.30
  75.5 147.0 %all-reduce.8.cloned.1.call-done = f32[2048,1024]{1,0:T(8,128)} async-done(((f32[2048,1024]{1,0:T(8,128)}), f32[2048,1024]{1,0:T(8,128)}) %all-reduce.8.cloned.1.call-update) | async-done | bytes 8388624 | tf_op jit(solution)/shard_map/psum | solution.py:57
  222.5 5.7 multiply_reduce_fusion.2
  228.2 3.4 copy-done.2
  231.6 16.3 %fusion.33 = f32[2048,2304]{1,0:T(8,128)} fusion(bf16[1024,2304]{1,0:T(8,128)(2,1)} %bitcast.27, f32[2048,1024]{1,0:T(8,128)S(1)} %get-tuple-element.26, f32[1024]{0:T(1024)S(1)} %convert_element_type.107, f32[2048]{0:T(1024)S(1)} %add_rsqrt_fusion), kind=kOutput, calls=%fused_computation.73 | convolution fusion | flops 9669967872 | bytes 31993856 | tf_op jit(solution)/shard_map/dot_general | solution.py:62
  247.9 11.3 %all-gather.6.cloned.1.call-done = bf16[2048,1024]{1,0:T(8,128)(2,1)} async-done(((bf16[2048,256]{1,0:T(8,128)(2,1)}), bf16[2048,1024]{1,0:T(8,128)(2,1)}) %all-gather.6.cloned.1.call-update) | async-done | bytes 4194320 | tf_op jit(solution)/shard_map/all_gather | solution.py:74
  259.2 18.2 %multiply_convert_fusion.1 = (bf16[2048,1152]{1,0:T(8,128)(2,1)}, bf16[2048,1152]{1,0:T(8,128)(2,1)}, bf16[2048,1152]{1,0:T(8,128)(2,1)}) fusion(f32[2048,2304]{1,0:T(8,128)} %fusion.33, bf16[2048,1024]{1,0:T(8,128)(2,1)} %all-gather.6.cloned.1.call-done, bf16[1152,1024]{1,0:T(8,128)(2,1)S(1)} %copy-done), kind=kOutput, calls=%fused_computation.5 | convolution fusion | flops 4869586944 | bytes 39583744 | tf_op jit(solution)/shard_map/dot_general | solution.py:75
  277.4 15.8 %fusion.4 = f32[2048,1024]{1,0:T(8,128)} fusion(bf16[1024,2304]{1,0:T(8,128)(2,1)} %bitcast.28, bf16[2048,1152]{1,0:T(8,128)(2,1)} %get-tuple-element.30, bf16[2048,1152]{1,0:T(8,128)(2,1)} %get-tuple-element.29), kind=kOutput, calls=%fused_computation.17 | convolution fusion | flops 9682550784 | bytes 22544384 | tf_op jit(solution)/shard_map/dot_general | solution.py:83
  293.5 152.8 %all-reduce.10.cloned.1.call-done = f32[2048,1024]{1,0:T(8,128)} async-done(((f32[2048,1024]{1,0:T(8,128)}), f32[2048,1024]{1,0:T(8,128)}) %all-reduce.10.cloned.1.call-update) | async-done | bytes 8388624 | tf_op jit(solution)/shard_map/psum | solution.py:84
  446.3 7.1 multiply_reduce_fusion
  454.5 5.9 multiply_add_fusion
  468.2 4.2 collective-permute-done.1
  476.1 5.1 convolution_convert_fusion.3
  483.8 50.9 %all-reduce.12.cloned.1.call-done = bf16[1024,3,256]{2,0,1:T(8,128)(2,1)} async-done(((bf16[1024,3,256]{2,0,1:T(8,128)(2,1)}), bf16[1024,3,256]{2,0,1:T(8,128)(2,1)}) %all-reduce.12.cloned.1.call-update) | async-done | bytes 1572880 | tf_op jit(solution)/shard_map/psum | solution.py:132
  534.8 9.6 convolution_convert_fusion.1
  544.6 16.9 %fusion.5 = bf16[1024,2304]{1,0:T(8,128)(2,1)} fusion(bf16[2048,1152]{1,0:T(8,128)(2,1)} %get-tuple-element.30, bf16[2048,1152]{1,0:T(8,128)(2,1)} %get-tuple-element.29, f32[2048,1024]{1,0:T(8,128)} %copy-done.2, f32[1024]{0:T(1024)S(1)} %convert_element_type.107, f32[2048]{0:T(1024)S(1)} %add_rsqrt_fusion), kind=kOutput, calls=%fused_computation.18 | convolution fusion | flops 9691201536 | bytes 22556672 | tf_op jit(solution)/shard_map/dot_general | solution.py:80
  561.6 10.1 %convert_element_type.131 = bf16[1024,2,1152]{2,1,0:T(2,128)(2,1)} reshape(bf16[1024,2304]{1,0:T(8,128)(2,1)} %fusion.5) | data formatting | bytes 9437184 | tf_op jit(solution)/shard_map/convert_element_type | solution.py:136
  571.6 9.4 convolution_convert_fusion
  581.0 5.5 fusion.23
  586.8 7.5 convolution_convert_fusion.2
  595.1 10.9 %all-reduce.14.cloned.1.call-done = bf16[1024,3,256]{2,0,1:T(8,128)(2,1)} async-done(((bf16[1024,3,256]{2,0,1:T(8,128)(2,1)}), bf16[1024,3,256]{2,0,1:T(8,128)(2,1)}) %all-reduce.14.cloned.1.call-update) | async-done | bytes 1572880 | tf_op jit(solution)/shard_map/psum | solution.py:132
  609.3 42.8 %reduce-scatter.3.cloned.1.call-done = bf16[2048,256]{1,0:T(8,128)(2,1)} async-done(((bf16[2048,1024]{1,0:T(8,128)(2,1)}), bf16[2048,256]{1,0:T(8,128)(2,1)}) %reduce-scatter.3.cloned.1.call-update) | async-done | bytes 1048592 | tf_op jit(solution)/shard_map/reduce_scatter | solution.py:67
  655.2 250.6 %all-reduce.16.cloned.1.call-done = (bf16[256,1024]{1,0:T(8,128)(2,1)}, bf16[1024,2,1152]{2,1,0:T(2,128)(2,1)}, bf16[1152,1024]{1,0:T(8,128)(2,1)}) async-done(((bf16[256,1024]{1,0:T(8,128)(2,1)}, bf16[1024,2,1152]{2,1,0:T(2,128)(2,1)}, bf16[1152,1024]{1,0:T(8,128)(2,1)}), (bf16[256,1024]{1,0:T(8,128)(2,1)}, bf16[1024,2,1152]{2,1,0:T(2,128)(2,1)}, ...) | async-done | bytes 7602192 | tf_op jit(solution)/shard_map/psum | solution.py:134
  905.8 7.3 convert_element_type.132
  917.2 34.8 %reduce-scatter.5.cloned.1.call-done = bf16[2048,256]{1,0:T(8,128)(2,1)} async-done(((bf16[2048,1024]{1,0:T(8,128)(2,1)}), bf16[2048,256]{1,0:T(8,128)(2,1)}) %reduce-scatter.5.cloned.1.call-update) | async-done | bytes 1048592 | tf_op jit(solution)/shard_map/reduce_scatter | solution.py:117
  954.1 21.5 %all-reduce = (bf16[256]{0:T(256)(128)(2,1)S(1)}, bf16[3,256]{1,0:T(4,128)(2,1)S(1)}, bf16[256]{0:T(256)(128)(2,1)S(1)}) all-reduce(bf16[256]{0:T(256)(128)(2,1)S(1)} %get-tuple-element.14, bf16[3,256]{1,0:T(4,128)(2,1)S(1)} %pad_maximum_fusion.10, ...), channel_id=1, replica_groups=mesh['dp'=2,'seq'=4,'chan'=4] {'dp','seq'}, use_global_device_ids=true, to_apply=%region_10.0 | all-reduce | flops 1280 | bytes 5120 | tf_op jit(solution)/shard_map/psum | solution.py:131
  977.3 6.1 psum.79
  (102 shorter events, 47.0 us)
Async XLA Ops:
  7.2 252.0 %copy-start = (bf16[1152,1024]{1,0:T(8,128)(2,1)S(1)}, bf16[1152,1024]{1,0:T(8,128)(2,1)}, u32[]{:S(2)}) copy-start(bf16[1152,1024]{1,0:T(8,128)(2,1)} %param.16) | copy-start | bytes 7077892
  7.2 3.4 copy-start.20
  7.2 40.1 %all-gather.4.cloned.1.call-start = ((), (), s32[]{:S(2)}) async-start(), calls=%async_computation.2 | async-start | bytes 5242880 | tf_op jit(solution)/shard_map/all_gather | solution.py:37
  7.9 214.5 %all-reduce.8.cloned.1.call-start = ((), (), s32[]{:S(2)}) async-start(), calls=%async_computation.3 | async-start | bytes 16777216 | tf_op jit(solution)/shard_map/psum | solution.py:57
  47.3 3.4 copy-start.7
  55.8 7.2 copy-start.4
  55.8 3.9 copy-start.18
  56.1 6.9 copy-start.5
  56.1 7.9 copy-start.14
  56.1 4.8 collective-permute-start
  68.6 190.6 %all-gather.6.cloned.1.call-start = ((), (), s32[]{:S(2)}) async-start(), calls=%async_computation.5 | async-start | bytes 5242880 | tf_op jit(solution)/shard_map/all_gather | solution.py:74
  69.4 376.9 %all-reduce.10.cloned.1.call-start = ((), (), s32[]{:S(2)}) async-start(), calls=%async_computation.6 | async-start | bytes 16777216 | tf_op jit(solution)/shard_map/psum | solution.py:84
  228.2 3.4 copy-start.2
  293.3 241.4 %all-reduce.12.cloned.1.call-start = ((), (), s32[]{:S(2)}) async-start(), calls=%async_computation.8 | async-start | bytes 3145728 | tf_op jit(solution)/shard_map/psum | solution.py:132
  446.3 8.2 copy-start.3
  446.3 18.4 %slice-start = ((s8[6291456]{0:T(1024)(128)(4,1)}), s8[4194304]{0:T(1024)(128)(4,1)S(1)}, s32[]{:S(2)}) async-start(s8[6291456]{0:T(1024)(128)(4,1)} %bitcast.24), calls=%async_computation.11 | async-start | bytes 8388608
  454.5 10.1 %slice-start.1 = ((s8[6291456]{0:T(1024)(128)(4,1)}), s8[2097152]{0:T(1024)(128)(4,1)S(1)}, s32[]{:S(2)}) async-start(s8[6291456]{0:T(1024)(128)(4,1)} %bitcast.24), calls=%async_computation.12 | async-start | bytes 4194304
  460.4 4.3 copy-start.1
  460.4 4.3 copy-start.6
  460.4 5.4 copy-start.12
  466.9 5.5 collective-permute-start.1
  473.2 8.0 copy-start.15
  473.2 2.9 copy-start.8
  473.5 7.6 copy-start.16
  483.8 122.2 %all-reduce.14.cloned.1.call-start = ((), (), s32[]{:S(2)}) async-start(), calls=%async_computation.9 | async-start | bytes 3145728 | tf_op jit(solution)/shard_map/psum | solution.py:132
  534.7 117.3 %reduce-scatter.3.cloned.1.call-start = ((), (), s32[]{:S(2)}) async-start(), calls=%async_computation.4 | async-start | bytes 5242880 | tf_op jit(solution)/shard_map/reduce_scatter | solution.py:67
  544.4 361.5 %all-reduce.16.cloned.1.call-start = ((), (), s32[]{:S(2)}) async-start(), calls=%async_computation.10 | async-start | bytes 15204352 | tf_op jit(solution)/shard_map/psum | solution.py:134
  571.6 9.4 copy-start.10
  586.5 365.4 %reduce-scatter.5.cloned.1.call-start = ((), (), s32[]{:S(2)}) async-start(), calls=%async_computation.7 | async-start | bytes 5242880 | tf_op jit(solution)/shard_map/reduce_scatter | solution.py:117
  905.8 7.3 copy-start.13
  913.1 3.0 copy-start.17
  913.1 38.8 %copy-start.11 = (bf16[2048,256]{1,0:T(8,128)(2,1)S(1)}, bf16[2048,256]{1,0:T(8,128)(2,1)}, u32[]{:S(2)}) copy-start(bf16[2048,256]{1,0:T(8,128)(2,1)} %param.9) | copy-start | bytes 3145732
  (3 other events, 3.0 us)
Sparse Core Ops, SparseCore 0:
  9.6 37.7 all-gather.3
  68.8 153.6 all-reduce.7
  224.0 35.1 all-gather.5
  293.4 152.8 all-reduce.9
  483.9 50.7 all-reduce.11
  536.9 68.9 all-reduce.13
  608.5 43.5 reduce-scatter.2
  657.1 248.6 all-reduce.15
  908.3 43.5 reduce-scatter.4
